TPU v7x, 32 devices: a whole 2x2x4 slice. The times are simulated.
32 devices in a mesh: dp: 8 (over y, x, core), fsdp: 4 (over z).
Axes of the slice: x: 2, y: 2, z: 4, core: 2. Of those that a mesh axis runs over, the one named last changes fastest.
Arguments:
- inputs: bfloat16 [32, 512, 1024], P(('dp', 'fsdp')), may hold values from -6 to 6
- segment_ids: int32 [32, 512], P(('dp', 'fsdp')), may hold values from 0 to 6, as said below
- query_weight: bfloat16 [1024, 1024], P(('dp', 'fsdp')), may hold values from -0.1875 to 0.1875
- key_weight: bfloat16 [1024, 1024], P(('dp', 'fsdp')), may hold values from -0.1875 to 0.1875
- value_weight: bfloat16 [1024, 1024], P(('dp', 'fsdp')), may hold values from -0.1875 to 0.1875
- output_weight: bfloat16 [1024, 1024], P(('dp', 'fsdp')), may hold values from -1 to 1
- query_bias: bfloat16 [1024], P(('dp', 'fsdp')), may hold values from -3 to 3
- value_bias: bfloat16 [1024], P(('dp', 'fsdp')), may hold values from -3 to 3
- output_bias: bfloat16 [1024], P(('dp', 'fsdp')), may hold values from -3 to 3
- attn_gain: bfloat16 [1024], P(('dp', 'fsdp')), may hold values from 0.5 to 1.5
- attn_shift: bfloat16 [1024], P(('dp', 'fsdp')), may hold values from -2 to 2
- inner_weight: bfloat16 [1024, 4096], P(('dp', 'fsdp')), may hold values from -0.1875 to 0.1875
- inner_bias: bfloat16 [4096], P(('dp', 'fsdp')), may hold values from -3 to 3
- outer_weight: bfloat16 [4096, 1024], P(('dp', 'fsdp')), may hold values from -0.125 to 0.125
- outer_bias: bfloat16 [1024], P(('dp', 'fsdp')), may hold values from -3 to 3
- ffn_gain: bfloat16 [1024], P(('dp', 'fsdp')), may hold values from 0.5 to 1.5
- ffn_shift: bfloat16 [1024], P(('dp', 'fsdp')), may hold values from -2 to 2
- out_grad: bfloat16 [32, 512, 1024], P(('dp', 'fsdp')), may hold values from -6 to 6
Outputs:
- outputs: bfloat16 [32, 512, 1024], P(('dp', 'fsdp'))
- input_grad: float32 [32, 512, 1024], P(('dp', 'fsdp'))
- grad_query_weight: float32 [1024, 1024], P(('dp', 'fsdp'))
- grad_key_weight: float32 [1024, 1024], P(('dp', 'fsdp'))
- grad_value_weight: float32 [1024, 1024], P(('dp', 'fsdp'))
- grad_output_weight: float32 [1024, 1024], P(('dp', 'fsdp'))
- grad_query_bias: float32 [1024], P(('dp', 'fsdp'))
- grad_value_bias: float32 [1024], P(('dp', 'fsdp'))
- grad_output_bias: float32 [1024], P(('dp', 'fsdp'))
- grad_attn_gain: float32 [1024], P(('dp', 'fsdp'))
- grad_attn_shift: float32 [1024], P(('dp', 'fsdp'))
- grad_inner_weight: float32 [1024, 4096], P(('dp', 'fsdp'))
- grad_inner_bias: float32 [4096], P(('dp', 'fsdp'))
- grad_outer_weight: float32 [4096, 1024], P(('dp', 'fsdp'))
- grad_outer_bias: float32 [1024], P(('dp', 'fsdp'))
- grad_ffn_gain: float32 [1024], P(('dp', 'fsdp'))
- grad_ffn_shift: float32 [1024], P(('dp', 'fsdp'))
Inputs may be any that keep to these rules, and one draw needn't show every extreme that they name: `segment_ids`: in each row the document numbers start at 1, never fall and rise by one at each new document, up to 6 documents; padding (0) is a tail of at most 128 positions.
All inputs are finite; a program needn't handle non-finite values.
Results may differ from a plain program's by a relative error of at most 0.014.
Values may be sent and summed in bfloat16 or wider, within the bound.
No kernel may reach another device: no remote copies, remote signals or barrier semaphores. Data moves between devices by JAX's collectives and lax.ppermute only.
A program may use at most 256 MiB of HBM per device.

v0:
```python
import jax
import jax.numpy as jnp
from jax import lax
from jax.sharding import PartitionSpec as P

H = 16
HD = 64
EPSILON = 1e-05


def scaled_norm(rows_in, gain):
    row_mean = jnp.mean(rows_in, axis=-1, keepdims=True)
    centred = rows_in - row_mean
    spread = jnp.mean(centred * centred, axis=-1, keepdims=True)
    return centred * lax.rsqrt(spread + EPSILON) * gain


def gelu_exact(value_in):
    return jax.nn.gelu(value_in, approximate=False)


def to_groups(matrix, row_count, seq_len):
    groups = H // 4
    shaped = matrix.reshape(row_count, seq_len, groups, 4, HD).transpose(0, 2, 1, 3, 4)
    return shaped.reshape(row_count * groups, seq_len, 4, HD)


def from_groups(stacked, row_count, seq_len):
    groups = stacked.shape[0] // row_count
    shaped = stacked.reshape(row_count, groups, seq_len, 4, HD).transpose(0, 2, 1, 3, 4)
    return shaped.reshape(row_count * seq_len, groups * 4 * HD)


def masked_scores(query_block, key_block, seg_row):
    score_scale = HD ** (-0.5)
    scores = (
        jnp.einsum("qhd,khd->hqk", query_block, key_block, preferred_element_type=jnp.float32)
        * score_scale
    )
    same_doc = seg_row[:, None] == seg_row[None, :]
    return jnp.where(same_doc[None], scores, -1e30)


def attend_forward(item_set):
    query_block, key_block, value_block, seg_row = item_set
    scores = masked_scores(query_block, key_block, seg_row)
    row_max = jnp.max(scores, axis=-1, keepdims=True)
    raised = jnp.exp(scores - row_max)
    row_total = jnp.sum(raised, axis=-1, keepdims=True)
    prob_low = (raised / row_total).astype(jnp.bfloat16)
    mixed_block = jnp.einsum(
        "hqk,khd->qhd", prob_low, value_block, preferred_element_type=jnp.float32
    )
    return (mixed_block, (row_max + jnp.log(row_total))[..., 0])


def attend_backward(item_set):
    query_block, key_block, value_block, seg_row, mixed_grad, log_total = item_set
    score_scale = HD ** (-0.5)
    scores = masked_scores(query_block, key_block, seg_row)
    probabilities = jnp.exp(scores - log_total[..., None])
    prob_low = probabilities.astype(jnp.bfloat16)
    value_grad = jnp.einsum(
        "hqk,qhd->khd", prob_low, mixed_grad, preferred_element_type=jnp.float32
    )
    prob_grad = jnp.einsum(
        "qhd,khd->hqk", mixed_grad, value_block, preferred_element_type=jnp.float32
    )
    inner_sum = jnp.sum(probabilities * prob_grad, axis=-1, keepdims=True)
    score_grad = (probabilities * (prob_grad - inner_sum)).astype(jnp.bfloat16)
    query_grad = (
        jnp.einsum("hqk,khd->qhd", score_grad, key_block, preferred_element_type=jnp.float32)
        * score_scale
    )
    key_grad = (
        jnp.einsum("hqk,qhd->khd", score_grad, query_block, preferred_element_type=jnp.float32)
        * score_scale
    )
    return (query_grad, key_grad, value_grad)


def matmul(left, right):
    return jnp.dot(left, right, preferred_element_type=jnp.float32)


def column_sum(matrix):
    return jnp.sum(matrix.astype(jnp.float32), axis=0)


def shards(
    inputs,
    segment_ids,
    query_weight,
    key_weight,
    value_weight,
    output_weight,
    query_bias,
    value_bias,
    output_bias,
    attn_gain,
    attn_shift,
    inner_weight,
    inner_bias,
    outer_weight,
    outer_bias,
    ffn_gain,
    ffn_shift,
    out_grad,
):
    row_count, seq_len, model_width = inputs.shape
    tokens_here = row_count * seq_len
    flattened = inputs.reshape(tokens_here, model_width)
    (
        query_full,
        key_full,
        value_full,
        output_full,
        query_bias_full,
        value_bias_full,
        output_bias_full,
        attn_gain_full,
        attn_shift_full,
    ) = (
        lax.all_gather(query_weight, ("dp", "fsdp"), axis=0, tiled=True),
        lax.all_gather(key_weight, ("dp", "fsdp"), axis=0, tiled=True),
        lax.all_gather(value_weight, ("dp", "fsdp"), axis=0, tiled=True),
        lax.all_gather(output_weight, ("dp", "fsdp"), axis=0, tiled=True),
        lax.all_gather(query_bias, ("dp", "fsdp"), axis=0, tiled=True),
        lax.all_gather(value_bias, ("dp", "fsdp"), axis=0, tiled=True),
        lax.all_gather(output_bias, ("dp", "fsdp"), axis=0, tiled=True),
        lax.all_gather(attn_gain, ("dp", "fsdp"), axis=0, tiled=True),
        lax.all_gather(attn_shift, ("dp", "fsdp"), axis=0, tiled=True),
    )
    queries = (matmul(flattened, query_full) + query_bias_full.astype(jnp.float32)).astype(
        jnp.bfloat16
    )
    key_rows = matmul(flattened, key_full).astype(jnp.bfloat16)
    value_rows = (matmul(flattened, value_full) + value_bias_full.astype(jnp.float32)).astype(
        jnp.bfloat16
    )
    query_groups = to_groups(queries, row_count, seq_len)
    key_groups = to_groups(key_rows, row_count, seq_len)
    value_groups = to_groups(value_rows, row_count, seq_len)
    seg_repeat = jnp.repeat(segment_ids, H // 4, axis=0)
    group_mixed, log_totals = lax.map(
        attend_forward, (query_groups, key_groups, value_groups, seg_repeat)
    )
    mixed_low = from_groups(group_mixed, row_count, seq_len).astype(jnp.bfloat16)
    attn_branch = matmul(mixed_low, output_full) + output_bias_full.astype(jnp.float32)
    attn_sum = flattened.astype(jnp.float32) + attn_branch
    attn_normed = scaled_norm(
        attn_sum, attn_gain_full.astype(jnp.float32)
    ) + attn_shift_full.astype(jnp.float32)
    normed_low = attn_normed.astype(jnp.bfloat16)
    inner_full, inner_bias_full, outer_full, outer_bias_full, ffn_gain_full, ffn_shift_full = (
        lax.all_gather(inner_weight, ("dp", "fsdp"), axis=0, tiled=True),
        lax.all_gather(inner_bias, ("dp", "fsdp"), axis=0, tiled=True),
        lax.all_gather(outer_weight, ("dp", "fsdp"), axis=0, tiled=True),
        lax.all_gather(outer_bias, ("dp", "fsdp"), axis=0, tiled=True),
        lax.all_gather(ffn_gain, ("dp", "fsdp"), axis=0, tiled=True),
        lax.all_gather(ffn_shift, ("dp", "fsdp"), axis=0, tiled=True),
    )
    inner_pre = matmul(normed_low, inner_full) + inner_bias_full.astype(jnp.float32)
    act_low = gelu_exact(inner_pre).astype(jnp.bfloat16)
    ffn_branch = matmul(act_low, outer_full) + outer_bias_full.astype(jnp.float32)
    ffn_sum = attn_normed + ffn_branch
    outputs = (
        scaled_norm(ffn_sum, ffn_gain_full.astype(jnp.float32)) + ffn_shift_full.astype(jnp.float32)
    ).astype(jnp.bfloat16)
    inner_back, outer_back, ffn_gain_back = (
        lax.all_gather(inner_weight, ("dp", "fsdp"), axis=0, tiled=True),
        lax.all_gather(outer_weight, ("dp", "fsdp"), axis=0, tiled=True),
        lax.all_gather(ffn_gain, ("dp", "fsdp"), axis=0, tiled=True),
    )
    grad_out = out_grad.reshape(tokens_here, model_width).astype(jnp.float32)
    _, ffn_norm_pull = jax.vjp(scaled_norm, ffn_sum, ffn_gain_back.astype(jnp.float32))
    grad_ffn_sum, grad_ffn_gain = ffn_norm_pull(grad_out)
    grad_ffn_shift = jnp.sum(grad_out, axis=0)
    branch_grad = grad_ffn_sum.astype(jnp.bfloat16)
    grad_outer_bias = column_sum(branch_grad)
    grad_outer = jnp.einsum("nf,nd->fd", act_low, branch_grad, preferred_element_type=jnp.float32)
    grad_act = jnp.einsum("nd,fd->nf", branch_grad, outer_back, preferred_element_type=jnp.float32)
    _, gelu_pull = jax.vjp(gelu_exact, inner_pre)
    inner_grad = gelu_pull(grad_act)[0].astype(jnp.bfloat16)
    grad_inner_bias = column_sum(inner_grad)
    grad_inner = jnp.einsum("nd,nf->df", normed_low, inner_grad, preferred_element_type=jnp.float32)
    grad_normed = grad_ffn_sum + jnp.einsum(
        "nf,df->nd", inner_grad, inner_back, preferred_element_type=jnp.float32
    )
    ffn_terms = (
        grad_inner,
        grad_inner_bias,
        grad_outer,
        grad_outer_bias,
        grad_ffn_gain,
        grad_ffn_shift,
    )
    ffn_owned = (
        lax.psum_scatter(ffn_terms[0], ("dp", "fsdp"), scatter_dimension=0, tiled=True),
        lax.psum_scatter(ffn_terms[1], ("dp", "fsdp"), scatter_dimension=0, tiled=True),
        lax.psum_scatter(ffn_terms[2], ("dp", "fsdp"), scatter_dimension=0, tiled=True),
        lax.psum_scatter(ffn_terms[3], ("dp", "fsdp"), scatter_dimension=0, tiled=True),
        lax.psum_scatter(ffn_terms[4], ("dp", "fsdp"), scatter_dimension=0, tiled=True),
        lax.psum_scatter(ffn_terms[5], ("dp", "fsdp"), scatter_dimension=0, tiled=True),
    )
    (
        shard_inner,
        shard_inner_bias,
        shard_outer,
        shard_outer_bias,
        shard_ffn_gain,
        shard_ffn_shift,
    ) = ffn_owned
    query_back, key_back, value_back, output_back, attn_gain_back = (
        lax.all_gather(query_weight, ("dp", "fsdp"), axis=0, tiled=True),
        lax.all_gather(key_weight, ("dp", "fsdp"), axis=0, tiled=True),
        lax.all_gather(value_weight, ("dp", "fsdp"), axis=0, tiled=True),
        lax.all_gather(output_weight, ("dp", "fsdp"), axis=0, tiled=True),
        lax.all_gather(attn_gain, ("dp", "fsdp"), axis=0, tiled=True),
    )
    _, attn_norm_pull = jax.vjp(scaled_norm, attn_sum, attn_gain_back.astype(jnp.float32))
    grad_attn_sum, grad_attn_gain = attn_norm_pull(grad_normed)
    grad_attn_shift = jnp.sum(grad_normed, axis=0)
    attn_grad = grad_attn_sum.astype(jnp.bfloat16)
    grad_output_bias = column_sum(attn_grad)
    grad_output = jnp.einsum("nd,ne->de", mixed_low, attn_grad, preferred_element_type=jnp.float32)
    mixed_grad = jnp.einsum(
        "ne,de->nd", attn_grad, output_back, preferred_element_type=jnp.float32
    ).astype(jnp.bfloat16)
    group_qgrad, group_kgrad, group_vgrad = lax.map(
        attend_backward,
        (
            query_groups,
            key_groups,
            value_groups,
            seg_repeat,
            to_groups(mixed_grad, row_count, seq_len),
            log_totals,
        ),
    )
    query_grad = from_groups(group_qgrad, row_count, seq_len).astype(jnp.bfloat16)
    key_grad = from_groups(group_kgrad, row_count, seq_len).astype(jnp.bfloat16)
    value_grad = from_groups(group_vgrad, row_count, seq_len).astype(jnp.bfloat16)
    grad_query_bias = column_sum(query_grad)
    grad_value_bias = column_sum(value_grad)
    grad_query = jnp.einsum("nd,ne->de", flattened, query_grad, preferred_element_type=jnp.float32)
    grad_key = jnp.einsum("nd,ne->de", flattened, key_grad, preferred_element_type=jnp.float32)
    grad_value = jnp.einsum("nd,ne->de", flattened, value_grad, preferred_element_type=jnp.float32)
    input_grad = (
        grad_attn_sum
        + jnp.einsum("ne,de->nd", query_grad, query_back, preferred_element_type=jnp.float32)
        + jnp.einsum("ne,de->nd", key_grad, key_back, preferred_element_type=jnp.float32)
        + jnp.einsum("ne,de->nd", value_grad, value_back, preferred_element_type=jnp.float32)
    )
    attn_owned = (
        lax.psum_scatter(grad_query, ("dp", "fsdp"), scatter_dimension=0, tiled=True),
        lax.psum_scatter(grad_key, ("dp", "fsdp"), scatter_dimension=0, tiled=True),
        lax.psum_scatter(grad_value, ("dp", "fsdp"), scatter_dimension=0, tiled=True),
        lax.psum_scatter(grad_output, ("dp", "fsdp"), scatter_dimension=0, tiled=True),
        lax.psum_scatter(grad_query_bias, ("dp", "fsdp"), scatter_dimension=0, tiled=True),
        lax.psum_scatter(grad_value_bias, ("dp", "fsdp"), scatter_dimension=0, tiled=True),
        lax.psum_scatter(grad_output_bias, ("dp", "fsdp"), scatter_dimension=0, tiled=True),
        lax.psum_scatter(grad_attn_gain, ("dp", "fsdp"), scatter_dimension=0, tiled=True),
        lax.psum_scatter(grad_attn_shift, ("dp", "fsdp"), scatter_dimension=0, tiled=True),
    )
    (
        shard_query,
        shard_key,
        shard_value,
        shard_output,
        shard_query_bias,
        shard_value_bias,
        shard_output_bias,
        shard_attn_gain,
        shard_attn_shift,
    ) = attn_owned
    return (
        outputs.reshape(row_count, seq_len, model_width),
        input_grad.reshape(row_count, seq_len, model_width),
        shard_query,
        shard_key,
        shard_value,
        shard_output,
        shard_query_bias,
        shard_value_bias,
        shard_output_bias,
        shard_attn_gain,
        shard_attn_shift,
        shard_inner,
        shard_inner_bias,
        shard_outer,
        shard_outer_bias,
        shard_ffn_gain,
        shard_ffn_shift,
    )


def solution(mesh):
    placed = (
        P(("dp", "fsdp"), None, None),
        P(("dp", "fsdp"), None),
        P(("dp", "fsdp"), None),
        P(("dp", "fsdp"), None),
        P(("dp", "fsdp"), None),
        P(("dp", "fsdp"), None),
        P(("dp", "fsdp")),
        P(("dp", "fsdp")),
        P(("dp", "fsdp")),
        P(("dp", "fsdp")),
        P(("dp", "fsdp")),
        P(("dp", "fsdp"), None),
        P(("dp", "fsdp")),
        P(("dp", "fsdp"), None),
        P(("dp", "fsdp")),
        P(("dp", "fsdp")),
        P(("dp", "fsdp")),
        P(("dp", "fsdp"), None, None),
    )
    return jax.shard_map(
        shards,
        mesh=mesh,
        in_specs=placed,
        out_specs=(
            P(("dp", "fsdp"), None, None),
            P(("dp", "fsdp"), None, None),
            P(("dp", "fsdp"), None),
            P(("dp", "fsdp"), None),
            P(("dp", "fsdp"), None),
            P(("dp", "fsdp"), None),
            P(("dp", "fsdp")),
            P(("dp", "fsdp")),
            P(("dp", "fsdp")),
            P(("dp", "fsdp")),
            P(("dp", "fsdp")),
            P(("dp", "fsdp"), None),
            P(("dp", "fsdp")),
            P(("dp", "fsdp"), None),
            P(("dp", "fsdp")),
            P(("dp", "fsdp")),
            P(("dp", "fsdp")),
        ),
        check_vma=False,
    )
```

profile of v0, /device:TPU:0, one launch (start us, length us, event | category | flops | bytes accessed | tf_op | source)
XLA Modules:
  0.0 1826.1 jit_solution(2462448369746053519)
XLA Ops:
  17.9 42.3 %all-reduce.18 = (bf16[1024]{0:T(1024)(128)(2,1)S(1)}, bf16[1024]{0:T(1024)(128)(2,1)S(1)}, bf16[1024]{0:T(1024)(128)(2,1)S(1)}, bf16[1024]{0:T(1024)(128)(2,1)S...) all-reduce(bf16[1024]{0:T(1024)(128)(2,1)S(1)} %dynamic-update-slic, ...), channel_id=1, replica_groups=mesh['dp'=8,'fsdp'=4] {'dp','fsdp'}, use_global_device_ids=true, to_apply=%add | all-reduce | flops 8192 | bytes 32768
  60.3 65.7 %all-gather = bf16[32,1,128]{2,1,0:T(2,128)(2,1)S(1)} all-gather(bf16[1,1,128]{2,1,0:T(2,128)(2,1)} %bitcast.239), channel_id=1, replica_groups=mesh['dp'=8,'fsdp'=4] {'dp','fsdp'}, dimensions={0}, use_global_device_ids=true | all-gather | bytes 8448 | tf_op jit(solution)/shard_map/all_gather | solution.py:157
  126.0 3.2 add_convert_fusion.3
  129.8 3.2 add_convert_fusion.2
  133.6 53.3 %all-gather.12.cloned.1.call-done = bf16[1024,1024]{1,0:T(8,128)(2,1)} async-done(((bf16[32,1024]{1,0:T(8,128)(2,1)}), bf16[1024,1024]{1,0:T(8,128)(2,1)}) %all-gather.12.cloned.1.call-update) | async-done | bytes 2097168 | tf_op jit(solution)/shard_map/all_gather | solution.py:125
  186.9 4.1 convolution_convert_fusion.1
  193.7 16.7 while.26
  210.3 34.8 %all-gather.14.cloned.1.call-done = bf16[1024,1024]{1,0:T(8,128)(2,1)} async-done(((bf16[32,1024]{1,0:T(8,128)(2,1)}), bf16[1024,1024]{1,0:T(8,128)(2,1)}) %all-gather.14.cloned.1.call-update) | async-done | bytes 2097168 | tf_op jit(solution)/shard_map/all_gather | solution.py:127
  245.1 3.5 fusion.82
  250.3 73.9 %all-gather.16.cloned.1.call-done = bf16[1024,4096]{1,0:T(8,128)(2,1)} async-done(((bf16[32,4096]{1,0:T(8,128)(2,1)}), bf16[1024,4096]{1,0:T(8,128)(2,1)}) %all-gather.16.cloned.1.call-update) | async-done | bytes 8388624 | tf_op jit(solution)/shard_map/all_gather | solution.py:156
  324.2 28.1 %multiply_convert_fusion.1 = (bf16[512,4096]{1,0:T(8,128)(2,1)}, f32[512,4096]{1,0:T(8,128)}, f32[512,4096]{1,0:T(8,128)}) fusion(f32[4096]{0:T(1024)S(1)} %bitcast.236, bf16[1024,4096]{1,0:T(8,128)(2,1)} %all-gather.16.cloned.1.call-done, f32[512,1024]{1,0:T(8,128)} %copy-done, f32[1024]{0:T(1024)S(1)} %convert_element_type.165, ...), kind=kOutput, calls=%fused_computation.66 | convolution fusion | flops 4436000768 | bytes 31485952 | tf_op jit(solution)/shard_map/dot_general | solution.py:83
  352.3 50.7 %all-gather.18.cloned.1.call-done = bf16[4096,1024]{1,0:T(8,128)(2,1)} async-done(((bf16[128,1024]{1,0:T(8,128)(2,1)}), bf16[4096,1024]{1,0:T(8,128)(2,1)}) %all-gather.18.cloned.1.call-update) | async-done | bytes 8388624 | tf_op jit(solution)/shard_map/all_gather | solution.py:158
  403.0 10.0 fusion.83
  416.4 15.4 convert_reduce_fusion
  431.8 8.9 multiply_reduce_fusion.1
  448.8 34.5 %while.27 = (s32[]{:T(128)}, bf16[4,512,4,64]{1,3,2,0:T(8,128)(2,1)}, bf16[4,512,4,64]{1,3,2,0:T(8,128)(2,1)}, bf16[4,512,4,64]{1,3,2,0:T(8,128)(2,1)S(1)}, bf16...) while((s32[]{:T(128)}, ...), condition=%wide.region_14.15_spmd, body=%wide.region_12.14_spmd.sunk | while | flops 687339520 | bytes 56954112 | solution.py:230
  483.4 4.7 convolution_bitcast_fusion.2
  488.1 5.3 copy.72
  494.9 3.2 convolution_bitcast_fusion.1
  498.1 5.4 copy.74
  503.6 3.2 convolution_bitcast_fusion
  506.7 5.4 copy.76
  513.4 4.4 fusion.86
  519.4 10.6 fusion.75
  531.3 10.4 fusion.87
  543.8 40.5 %all-reduce.17 = (f32[1024]{0:T(1024)S(1)}, f32[1024]{0:T(1024)S(1)}, f32[1024]{0:T(1024)S(1)}, f32[1024]{0:T(1024)S(1)}, f32[1024]{0:T(1024)S(1)}, /*index=5*/f...) all-reduce(f32[1024]{0:T(1024)S(1)} %reduce_sum.191, ...), channel_id=6, replica_groups=mesh['dp'=8,'fsdp'=4] {'dp','fsdp'}, use_global_device_ids=true, to_apply=%region_20.21.clone | all-reduce | flops 12288 | bytes 98304
  597.7 42.6 %reduce-scatter.19.cloned.1.call-done = f32[32,1024]{1,0:T(8,128)} async-done(((f32[1024,1024]{1,0:T(8,128)}), f32[32,1024]{1,0:T(8,128)}) %reduce-scatter.19.cloned.1.call-update) | async-done | bytes 131088
  640.3 149.2 %reduce-scatter.21.cloned.1.call-done = f32[32,1024]{1,0:T(8,128)} async-done(((f32[1024,1024]{1,0:T(8,128)}), f32[32,1024]{1,0:T(8,128)}) %reduce-scatter.21.cloned.1.call-update) | async-done | bytes 131088
  789.6 149.7 %reduce-scatter.23.cloned.1.call-done = f32[32,1024]{1,0:T(8,128)} async-done(((f32[1024,1024]{1,0:T(8,128)}), f32[32,1024]{1,0:T(8,128)}) %reduce-scatter.23.cloned.1.call-update) | async-done | bytes 131088
  939.3 149.4 %reduce-scatter.13.cloned.1.call-done = f32[32,1024]{1,0:T(8,128)} async-done(((f32[1024,1024]{1,0:T(8,128)}), f32[32,1024]{1,0:T(8,128)}) %reduce-scatter.13.cloned.1.call-update) | async-done | bytes 131088 | tf_op jit(solution)/shard_map/reduce_scatter | solution.py:259
  1088.7 365.5 %reduce-scatter.15.cloned.1.call-done = f32[32,4096]{1,0:T(8,128)} async-done(((f32[1024,4096]{1,0:T(8,128)}), f32[32,4096]{1,0:T(8,128)}) %reduce-scatter.15.cloned.1.call-update) | async-done | bytes 524304 | tf_op jit(solution)/shard_map/reduce_scatter | solution.py:199
  1454.2 364.9 %reduce-scatter.17.cloned.1.call-done = f32[128,1024]{1,0:T(8,128)} async-done(((f32[4096,1024]{1,0:T(8,128)}), f32[128,1024]{1,0:T(8,128)}) %reduce-scatter.17.cloned.1.call-update) | async-done | bytes 524304 | tf_op jit(solution)/shard_map/reduce_scatter | solution.py:201
  (233 shorter events, 98.7 us)
Async XLA Ops:
  7.2 118.9 %all-gather.8.cloned.1.call-start = ((), (), s32[]{:S(2)}) async-start(), calls=%async_computation.6 | async-start | bytes 2162688 | tf_op jit(solution)/shard_map/all_gather | solution.py:126
  7.9 121.9 %all-gather.10.cloned.1.call-start = ((), (), s32[]{:S(2)}) async-start(), calls=%async_computation.7 | async-start | bytes 2162688 | tf_op jit(solution)/shard_map/all_gather | solution.py:124
  8.7 178.3 %all-gather.12.cloned.1.call-start = ((), (), s32[]{:S(2)}) async-start(), calls=%async_computation.8 | async-start | bytes 2162688 | tf_op jit(solution)/shard_map/all_gather | solution.py:125
  9.4 235.7 %all-gather.14.cloned.1.call-start = ((), (), s32[]{:S(2)}) async-start(), calls=%async_computation.9 | async-start | bytes 2162688 | tf_op jit(solution)/shard_map/all_gather | solution.py:127
  10.0 314.2 %all-gather.16.cloned.1.call-start = ((), (), s32[]{:S(2)}) async-start(), calls=%async_computation.10 | async-start | bytes 8650752 | tf_op jit(solution)/shard_map/all_gather | solution.py:156
  10.6 392.4 %all-gather.18.cloned.1.call-start = ((), (), s32[]{:S(2)}) async-start(), calls=%async_computation.11 | async-start | bytes 8650752 | tf_op jit(solution)/shard_map/all_gather | solution.py:158
  11.1 629.2 %reduce-scatter.19.cloned.1.call-start = ((), (), s32[]{:S(2)}) async-start(), calls=%async_computation.15 | async-start | bytes 4325376
  133.6 59.0 %copy-start.23 = (s32[1,512]{1,0:T(1,128)S(1)}, s32[1,512]{1,0:T(1,128)}, u32[]{:S(2)}) copy-start(s32[1,512]{1,0:T(1,128)} %param.23) | copy-start | bytes 6148
  210.3 40.0 %copy-start.7 = (bf16[4,512,4,64]{1,3,2,0:T(8,128)(2,1)}, bf16[4,512,4,64]{1,3,2,0:T(8,128)(2,1)S(1)}, u32[]{:S(2)}) copy-start(bf16[4,512,4,64]{1,3,2,0:T(8,128)(2,1)S(1)} %get-tuple-element.439) | copy-start | bytes 3145732
  403.0 10.4 copy-start.5
  416.3 15.4 copy-start.14
  416.3 15.4 copy-start.1
  440.7 3.2 copy-start.12
  453.0 2.1 copy-start.9
  455.0 1.5 copy-start.19
  461.5 2.1 copy-start.9
  470.0 2.1 copy-start.9
  472.1 1.5 copy-start.19
  478.5 2.1 copy-start.9
  480.6 1.5 copy-start.19
  493.4 1.5 copy-start.22
  493.4 296.1 %reduce-scatter.21.cloned.1.call-start = ((), (), s32[]{:S(2)}) async-start(), calls=%async_computation.16 | async-start | bytes 4325376
  503.5 435.8 %reduce-scatter.23.cloned.1.call-start = ((), (), s32[]{:S(2)}) async-start(), calls=%async_computation.17 | async-start | bytes 4325376
  512.2 576.5 %reduce-scatter.13.cloned.1.call-start = ((), (), s32[]{:S(2)}) async-start(), calls=%async_computation.12 | async-start | bytes 4325376 | tf_op jit(solution)/shard_map/reduce_scatter | solution.py:259
  517.8 1.6 copy-start.2
  517.9 936.3 %reduce-scatter.15.cloned.1.call-start = ((), (), s32[]{:S(2)}) async-start(), calls=%async_computation.13 | async-start | bytes 17301504 | tf_op jit(solution)/shard_map/reduce_scatter | solution.py:199
  530.1 1289.0 %reduce-scatter.17.cloned.1.call-start = ((), (), s32[]{:S(2)}) async-start(), calls=%async_computation.14 | async-start | bytes 17301504 | tf_op jit(solution)/shard_map/reduce_scatter | solution.py:201
  541.7 1.6 copy-start.11
  589.6 3.1 copy-start.21
  589.6 3.1 copy-start.24
  592.6 1.6 copy-start.4
  592.6 2.2 copy-start.13
  (20 other events, 24.2 us)
Sparse Core Ops, SparseCore 0:
  10.9 59.3 all-gather.7
  73.2 55.3 all-gather.9
  131.6 55.3 all-gather.11
  189.7 55.3 all-gather.13
  247.9 76.2 all-gather.15
  327.0 75.9 all-gather.17
  493.6 146.7 reduce-scatter.18
  643.2 146.3 reduce-scatter.20
  792.4 146.8 reduce-scatter.22
  942.0 146.7 reduce-scatter.12
  1091.6 362.5 reduce-scatter.14
  1456.9 362.1 reduce-scatter.16
where the time goes:
time: 1840 us; the launch traced here: 1830 us
  waiting for transfers between devices  1440 us (78%)
  matrix products  156 us (8%)
  blocking collectives  149 us (8%)
  local copies, waits for them, and re-layouts  51.7 us (3%)
    reduce_scatter x1, waiting for transfers between devices, shards(): lax.psum_scatter(ffn_terms[0], ('dp', 'fsdp'), scatter_dimension=0, tiled...  365 us
    reduce_scatter x1, waiting for transfers between devices, shards(): lax.psum_scatter(ffn_terms[2], ('dp', 'fsdp'), scatter_dimension=0, tiled...  365 us
    unnamed x15, waiting for transfers between devices  345 us
    reduce_scatter x1, waiting for transfers between devices, shards(): lax.psum_scatter(grad_output, ('dp', 'fsdp'), scatter_dimension=0, tiled=...  149 us
    unnamed x2, blocking collectives  82.8 us
    all_gather x1, waiting for transfers between devices, shards(): lax.all_gather(inner_weight, ('dp', 'fsdp'), axis=0, tiled=True)  73.9 us
    all_gather x1, blocking collectives, shards(): lax.all_gather(inner_bias, ('dp', 'fsdp'), axis=0, tiled=True)  65.7 us
    all_gather x1, waiting for transfers between devices, shards(): lax.all_gather(key_weight, ('dp', 'fsdp'), axis=0, tiled=True)  53.3 us
  transfers between devices with their start and end apart: 12, of which 10 were waited for; matrix products, arithmetic and copies ran while one was open for 7% of the time, Pallas kernels for 0%

commit v1 on v0

--- a/solution.py
+++ b/solution.py
@@ -6,6 +6,18 @@
 H = 16
 HD = 64
 EPSILON = 1e-05
+
+
+def doubled_up(array, axis, dim):
+    ways, here = (lax.axis_size(axis), lax.axis_index(axis))
+    grown, reach = (array, 1)
+    while reach < ways:
+        theirs = lax.ppermute(grown, axis, [(d, d ^ reach) for d in range(ways)])
+        mine_first = jnp.concatenate([grown, theirs], axis=dim)
+        theirs_first = jnp.concatenate([theirs, grown], axis=dim)
+        grown = jnp.where(here & reach == 0, mine_first, theirs_first)
+        reach = 2 * reach
+    return grown
 
 
 def scaled_norm(rows_in, gain):
@@ -122,7 +134,7 @@
         attn_shift_full,
     ) = (
         lax.all_gather(query_weight, ("dp", "fsdp"), axis=0, tiled=True),
-        lax.all_gather(key_weight, ("dp", "fsdp"), axis=0, tiled=True),
+        doubled_up(key_weight, ("dp", "fsdp"), 0),
         lax.all_gather(value_weight, ("dp", "fsdp"), axis=0, tiled=True),
         lax.all_gather(output_weight, ("dp", "fsdp"), axis=0, tiled=True),
         lax.all_gather(query_bias, ("dp", "fsdp"), axis=0, tiled=True),

time: 1840 us -> 1750 us (0.951)
  waiting for transfers between devices: 1440 us -> 1310 us
  matrix products: 156 us -> 175 us
    reduce_scatter x1, waiting for transfers between devices: 149 us -> 0.01 us  [shards(): lax.psum_scatter(grad_output, ('dp', 'fsdp'), scatter_dimension=0, tiled=...]
    unnamed x15, waiting for transfers between devices: 345 us -> 448 us
    all_gather x1, waiting for transfers between devices: 53.3 us -> 0.01 us  [shards(): lax.all_gather(key_weight, ('dp', 'fsdp'), axis=0, tiled=True)]
    all_gather x1, waiting for transfers between devices: 34.8 us -> 0.01 us  [shards(): lax.all_gather(output_weight, ('dp', 'fsdp'), axis=0, tiled=True)]
    ppermute x0 -> x5, waiting for transfers between devices: none -> 22.5 us  [doubled_up(): theirs = lax.ppermute(grown, axis, [(d, d ^ reach) for d in range(ways)])]
    unnamed x68 -> x78, local copies, waits for them, and re-layouts: 39.2 us -> 30.6 us
  transfers between devices with their start and end apart: 12 -> 17, of which waited for: 10 -> 11; matrix products, arithmetic and copies ran while one was open for 7% -> 13% of each run, Pallas kernels for 0% -> 0%
where the time goes in v1:
time: 1750 us; the launch traced here: 1740 us
  waiting for transfers between devices  1310 us (75%)
  matrix products  175 us (10%)
  blocking collectives  165 us (9%)
  local copies, waits for them, and re-layouts  43.9 us (3%)
  other arithmetic  18.6 us (1%)
    unnamed x15, waiting for transfers between devices  448 us
    reduce_scatter x1, waiting for transfers between devices, shards(): lax.psum_scatter(ffn_terms[0], ('dp', 'fsdp'), scatter_dimension=0, tiled...  365 us
    reduce_scatter x1, waiting for transfers between devices, shards(): lax.psum_scatter(ffn_terms[2], ('dp', 'fsdp'), scatter_dimension=0, tiled...  365 us
    unnamed x2, blocking collectives  101 us
    all_gather x1, blocking collectives, shards(): lax.all_gather(inner_bias, ('dp', 'fsdp'), axis=0, tiled=True)  64.9 us
    all_gather x1, waiting for transfers between devices, shards(): lax.all_gather(inner_weight, ('dp', 'fsdp'), axis=0, tiled=True)  61.7 us
    all_gather x1, waiting for transfers between devices, shards(): lax.all_gather(outer_weight, ('dp', 'fsdp'), axis=0, tiled=True)  51.3 us
    dot_general x6, matrix products, matmul(): return jnp.dot(left, right, preferred_element_type=jnp.float32)  48.5 us
  transfers between devices with their start and end apart: 17, of which 11 were waited for; matrix products, arithmetic and copies ran while one was open for 13% of the time, Pallas kernels for 0%

profile of v1, /device:TPU:0, one launch (start us, length us, event | category | flops | bytes accessed | tf_op | source)
XLA Modules:
  0.0 1741.9 jit_solution(13887695356112175459)
XLA Ops:
  10.7 3.1 collective-permute-start
  17.2 3.1 collective-permute-start.1
  20.3 5.2 collective-permute-done.1
  28.9 13.3 collective-permute-done.3
  46.3 59.7 %all-reduce.18 = (bf16[1024]{0:T(1024)(128)(2,1)S(1)}, bf16[1024]{0:T(1024)(128)(2,1)S(1)}, bf16[1024]{0:T(1024)(128)(2,1)S(1)}, bf16[1024]{0:T(1024)(128)(2,1)S...) all-reduce(bf16[1024]{0:T(1024)(128)(2,1)S(1)} %dynamic-update-slic, ...), channel_id=1, replica_groups=mesh['dp'=8,'fsdp'=4] {'dp','fsdp'}, use_global_device_ids=true, to_apply=%add | all-reduce | flops 8192 | bytes 32768
  106.1 64.9 %all-gather = bf16[32,1,128]{2,1,0:T(2,128)(2,1)S(1)} all-gather(bf16[1,1,128]{2,1,0:T(2,128)(2,1)S(1)} %bitcast.238), channel_id=1, replica_groups=mesh['dp'=8,'fsdp'=4] {'dp','fsdp'}, dimensions={0}, use_global_device_ids=true | all-gather | bytes 8448 | tf_op jit(solution)/shard_map/all_gather | solution.py:169
  182.8 20.6 %while.26 = (s32[]{:T(128)}, bf16[4,512,4,64]{1,3,2,0:T(8,128)(2,1)}, f32[4,4,512]{2,1,0:T(4,128)S(1)}, bf16[4,512,4,64]{1,3,2,0:T(8,128)(2,1)}, s32[4,512]{1,0:...) while((s32[]{:T(128)}, ...), condition=%wide.region_3.4_spmd, body=%wide.region_0.3_spmd.sunk | while | flops 281278464 | bytes 15016029 | solution.py:157
  204.4 3.5 fusion.91
  208.3 61.7 %all-gather.14.cloned.1.call-done = bf16[1024,4096]{1,0:T(8,128)(2,1)} async-done(((bf16[32,4096]{1,0:T(8,128)(2,1)}), bf16[1024,4096]{1,0:T(8,128)(2,1)}) %all-gather.14.cloned.1.call-update) | async-done | bytes 8388624 | tf_op jit(solution)/shard_map/all_gather | solution.py:168
  270.1 27.7 %multiply_convert_fusion.1 = (bf16[512,4096]{1,0:T(8,128)(2,1)}, f32[512,4096]{1,0:T(8,128)}, f32[512,4096]{1,0:T(8,128)}) fusion(f32[4096]{0:T(1024)S(1)} %bitcast.235, bf16[1024,4096]{1,0:T(8,128)(2,1)} %all-gather.14.cloned.1.call-done, f32[512,1024]{1,0:T(8,128)S(1)} %get-tuple-element.239, f32[1024]{0:T(1024)S(1)} %convert_element_type.169, ...), kind=kOutput, calls=%fused_computation.66 | convolution fusion | flops 4436000768 | bytes 31485952 | tf_op jit(solution)/shard_map/dot_general | solution.py:95
  297.7 51.3 %all-gather.16.cloned.1.call-done = bf16[4096,1024]{1,0:T(8,128)(2,1)} async-done(((bf16[128,1024]{1,0:T(8,128)(2,1)}), bf16[4096,1024]{1,0:T(8,128)(2,1)}) %all-gather.16.cloned.1.call-update) | async-done | bytes 8388624 | tf_op jit(solution)/shard_map/all_gather | solution.py:170
  349.0 8.7 fusion.92
  361.1 13.8 convert_reduce_fusion
  374.9 9.1 multiply_reduce_fusion.1
  392.3 4.7 fusion.95
  400.4 44.7 %while.27 = (s32[]{:T(128)}, bf16[4,512,4,64]{1,3,2,0:T(8,128)(2,1)}, bf16[4,512,4,64]{1,3,2,0:T(8,128)(2,1)}, bf16[4,512,4,64]{1,3,2,0:T(8,128)(2,1)}, bf16[4,5...) while((s32[]{:T(128)}, ...), condition=%wide.region_14.15_spmd, body=%wide.region_12.14_spmd.sunk | while | flops 687339520 | bytes 56954112 | solution.py:242
  445.2 4.8 convolution_bitcast_fusion.2
  449.9 5.4 copy.69
  456.5 4.4 convolution_bitcast_fusion.1
  461.0 5.3 copy.71
  466.4 4.8 convolution_bitcast_fusion
  471.2 5.4 copy.73
  476.6 10.7 fusion.84
  488.5 10.4 fusion.96
  502.3 40.9 %all-reduce.17 = (f32[1024]{0:T(1024)S(1)}, f32[1024]{0:T(1024)S(1)}, f32[1024]{0:T(1024)S(1)}, f32[1024]{0:T(1024)S(1)}, f32[1024]{0:T(1024)S(1)}, /*index=5*/f...) all-reduce(f32[1024]{0:T(1024)S(1)} %reduce_sum.191, ...), channel_id=6, replica_groups=mesh['dp'=8,'fsdp'=4] {'dp','fsdp'}, use_global_device_ids=true, to_apply=%region_20.21.clone | all-reduce | flops 12288 | bytes 98304
  548.4 4.2 fusion.93
  556.1 4.1 add_bitcast_fusion
  560.2 146.0 %reduce-scatter.19.cloned.1.call-done = f32[32,1024]{1,0:T(8,128)} async-done(((f32[1024,1024]{1,0:T(8,128)}), f32[32,1024]{1,0:T(8,128)}) %reduce-scatter.19.cloned.1.call-update) | async-done | bytes 131088
  706.2 149.5 %reduce-scatter.21.cloned.1.call-done = f32[32,1024]{1,0:T(8,128)} async-done(((f32[1024,1024]{1,0:T(8,128)}), f32[32,1024]{1,0:T(8,128)}) %reduce-scatter.21.cloned.1.call-update) | async-done | bytes 131088
  855.7 149.1 %reduce-scatter.23.cloned.1.call-done = f32[32,1024]{1,0:T(8,128)} async-done(((f32[1024,1024]{1,0:T(8,128)}), f32[32,1024]{1,0:T(8,128)}) %reduce-scatter.23.cloned.1.call-update) | async-done | bytes 131088
  1004.8 365.2 %reduce-scatter.15.cloned.1.call-done = f32[32,4096]{1,0:T(8,128)} async-done(((f32[1024,4096]{1,0:T(8,128)}), f32[32,4096]{1,0:T(8,128)}) %reduce-scatter.15.cloned.1.call-update) | async-done | bytes 524304 | tf_op jit(solution)/shard_map/reduce_scatter | solution.py:211
  1370.0 364.9 %reduce-scatter.17.cloned.1.call-done = f32[128,1024]{1,0:T(8,128)} async-done(((f32[4096,1024]{1,0:T(8,128)}), f32[128,1024]{1,0:T(8,128)}) %reduce-scatter.17.cloned.1.call-update) | async-done | bytes 524304 | tf_op jit(solution)/shard_map/reduce_scatter | solution.py:213
  (256 shorter events, 121.5 us)
Async XLA Ops:
  7.2 37.2 %copy-start.21 = (bf16[32]{0:T(256)(128)(2,1)S(1)}, bf16[32]{0:T(256)(128)(2,1)}, u32[]{:S(2)}) copy-start(bf16[32]{0:T(256)(128)(2,1)} %param.29) | copy-start | bytes 196
  7.2 37.5 %copy-start.22 = (bf16[32]{0:T(256)(128)(2,1)S(1)}, bf16[32]{0:T(256)(128)(2,1)}, u32[]{:S(2)}) copy-start(bf16[32]{0:T(256)(128)(2,1)} %param.28) | copy-start | bytes 196
  7.2 37.7 %copy-start.23 = (bf16[32]{0:T(256)(128)(2,1)S(1)}, bf16[32]{0:T(256)(128)(2,1)}, u32[]{:S(2)}) copy-start(bf16[32]{0:T(256)(128)(2,1)} %param.30) | copy-start | bytes 196
  7.2 37.9 %copy-start.24 = (bf16[32]{0:T(256)(128)(2,1)S(1)}, bf16[32]{0:T(256)(128)(2,1)}, u32[]{:S(2)}) copy-start(bf16[32]{0:T(256)(128)(2,1)} %param.31) | copy-start | bytes 196
  7.2 38.2 %copy-start.25 = (bf16[32]{0:T(256)(128)(2,1)S(1)}, bf16[32]{0:T(256)(128)(2,1)}, u32[]{:S(2)}) copy-start(bf16[32]{0:T(256)(128)(2,1)} %param.32) | copy-start | bytes 196
  7.2 38.4 %copy-start.26 = (bf16[32]{0:T(256)(128)(2,1)S(1)}, bf16[32]{0:T(256)(128)(2,1)}, u32[]{:S(2)}) copy-start(bf16[32]{0:T(256)(128)(2,1)} %param.36) | copy-start | bytes 196
  7.2 38.6 %copy-start.27 = (bf16[32]{0:T(256)(128)(2,1)S(1)}, bf16[32]{0:T(256)(128)(2,1)}, u32[]{:S(2)}) copy-start(bf16[32]{0:T(256)(128)(2,1)} %param.37) | copy-start | bytes 196
  7.3 38.8 %copy-start.28 = (bf16[32]{0:T(256)(128)(2,1)S(1)}, bf16[32]{0:T(256)(128)(2,1)}, u32[]{:S(2)}) copy-start(bf16[32]{0:T(256)(128)(2,1)} %param.38) | copy-start | bytes 196
  7.3 98.8 %copy-start.20 = (bf16[128]{0:T(256)(128)(2,1)S(1)}, bf16[128]{0:T(256)(128)(2,1)}, u32[]{:S(2)}) copy-start(bf16[128]{0:T(256)(128)(2,1)} %param.34) | copy-start | bytes 772
  7.3 163.8 %copy-start.18 = (bf16[1,512,1024]{2,1,0:T(8,128)(2,1)S(1)}, bf16[1,512,1024]{2,1,0:T(8,128)(2,1)}, u32[]{:S(2)}) copy-start(bf16[1,512,1024]{2,1,0:T(8,128)(2,1)} %param.22) | copy-start | bytes 3145732
  7.3 166.7 %all-gather.8.cloned.1.call-start = ((), (), s32[]{:S(2)}) async-start(), calls=%async_computation.6 | async-start | bytes 2162688 | tf_op jit(solution)/shard_map/all_gather | solution.py:138
  8.0 170.3 %all-gather.10.cloned.1.call-start = ((), (), s32[]{:S(2)}) async-start(), calls=%async_computation.7 | async-start | bytes 2162688 | tf_op jit(solution)/shard_map/all_gather | solution.py:136
  8.8 194.6 %all-gather.12.cloned.1.call-start = ((), (), s32[]{:S(2)}) async-start(), calls=%async_computation.8 | async-start | bytes 2162688 | tf_op jit(solution)/shard_map/all_gather | solution.py:139
  9.5 260.6 %all-gather.14.cloned.1.call-start = ((), (), s32[]{:S(2)}) async-start(), calls=%async_computation.9 | async-start | bytes 8650752 | tf_op jit(solution)/shard_map/all_gather | solution.py:168
  10.1 339.0 %all-gather.16.cloned.1.call-start = ((), (), s32[]{:S(2)}) async-start(), calls=%async_computation.10 | async-start | bytes 8650752 | tf_op jit(solution)/shard_map/all_gather | solution.py:170
  10.7 541.9 %all-gather.18.cloned.1.call-start = ((), (), s32[]{:S(2)}) async-start(), calls=%async_computation.11 | async-start | bytes 2162688 | tf_op jit(solution)/shard_map/all_gather | solution.py:228
  10.7 5.5 collective-permute-start
  17.2 8.3 collective-permute-start.1
  25.6 1.6 collective-permute-start.2
  27.3 14.9 collective-permute-start.3
  42.7 128.3 %collective-permute-start.4 = (bf16[512,1024]{1,0:T(8,128)(2,1)S(1)}, bf16[512,1024]{1,0:T(8,128)(2,1)}, u32[]{:S(2)}, u32[]{:S(2)}) collective-permute-start(bf16[512,1024]{1,0:T(8,128)(2,1)S(1)} %maximum_select_fusion.4), channel_id=1, source_target_pairs={{0,16},{1,17},{2,18},{3,19},{4,20},{5,21},{6,22},{7,23},{8,24},{9,... | collective-permute-start | bytes 3145736 | tf_op jit(solution)/shard_map/ppermute | solution.py:15
  44.3 515.9 %reduce-scatter.13.cloned.1.call-start = ((), (), s32[]{:S(2)}) async-start(), calls=%async_computation.12 | async-start | bytes 4325376 | tf_op jit(solution)/shard_map/reduce_scatter | solution.py:271
  178.3 3.4 copy-start.19
  349.0 9.1 copy-start.3
  361.1 13.8 copy-start.12
  374.9 9.1 copy-start.29
  397.0 309.2 %reduce-scatter.19.cloned.1.call-start = ((), (), s32[]{:S(2)}) async-start(), calls=%async_computation.15 | async-start | bytes 4325376
  455.3 400.4 %reduce-scatter.21.cloned.1.call-start = ((), (), s32[]{:S(2)}) async-start(), calls=%async_computation.16 | async-start | bytes 4325376
  466.3 538.5 %reduce-scatter.23.cloned.1.call-start = ((), (), s32[]{:S(2)}) async-start(), calls=%async_computation.17 | async-start | bytes 4325376
  476.6 893.4 %reduce-scatter.15.cloned.1.call-start = ((), (), s32[]{:S(2)}) async-start(), calls=%async_computation.13 | async-start | bytes 17301504 | tf_op jit(solution)/shard_map/reduce_scatter | solution.py:211
  487.3 1247.6 %reduce-scatter.17.cloned.1.call-start = ((), (), s32[]{:S(2)}) async-start(), calls=%async_computation.14 | async-start | bytes 17301504 | tf_op jit(solution)/shard_map/reduce_scatter | solution.py:213
  552.6 3.5 copy-start.11
  (30 other events, 53.9 us)
Sparse Core Ops, SparseCore 0:
  11.1 63.1 all-gather.7
  77.1 55.4 all-gather.9
  135.6 55.3 all-gather.11
  193.8 76.2 all-gather.13
  272.8 76.1 all-gather.15
  351.8 55.0 all-gather.17
  409.8 146.8 reduce-scatter.12
  559.6 146.6 reduce-scatter.18
  709.1 146.5 reduce-scatter.20
  858.4 146.3 reduce-scatter.22
  1007.7 362.2 reduce-scatter.14
  1372.7 362.1 reduce-scatter.16
